TPU v7x, 128 devices: a whole 4x4x4 slice. The times are simulated.
128 devices in a mesh: req: 32 (over z, y, x_lo), exp: 4 (over x_hi, core).
Axes of the slice: x: 4 (x_hi: 2, x_lo: 2; x = x_hi * 2 + x_lo), y: 4, z: 4, core: 2. Of those that a mesh axis runs over, the one named last changes fastest.
Arguments:
- hidden_in: bfloat16 [8192, 2048], P(('req', 'exp')), may hold values from -6 to 6
- query_in: bfloat16 [8192, 2048], P('req', 'exp'), may hold values from -6 to 6
- key_in: bfloat16 [8192, 2048], P('req', 'exp'), may hold values from -6 to 6
- value_in: bfloat16 [8192, 2048], P('req', 'exp'), may hold values from -24 to 24
- query_gain: float32 [128], replicated, may hold values from 0.5 to 2.5
- key_gain: float32 [128], replicated, may hold values from 0.5 to 2.5
- cache_keys: bfloat16 [64, 32, 2048], P('req', None, 'exp'), may hold values from -400 to 400
- cache_values: bfloat16 [64, 32, 2048], P('req', None, 'exp'), may hold values from -24 to 24
- cache_block: int32 [128], replicated, may hold values from -1 to 63, as said below
- request_lengths: int32 [32, 4], P('req'), may hold values from 1 to 128, 256 in all within a row
- out_proj: bfloat16 [2048, 2048], P('exp'), may hold values from -0.125 to 0.125
- norm_gain: float32 [2048], replicated, may hold values from 0.25 to 1.75
- expert_ids: int32 [8192, 8], P(('req', 'exp')), may hold values from 0 to 63, all different within a row; in each aligned block of 64 rows (0 to 63, 64 to 127, ...) at most 10 rows name the same one
- gate_values: float32 [8192, 8], P(('req', 'exp')), may hold values from 0.4 to 1.6
- old_slots: int32 [64], replicated, may hold values from 0 to 63, each once
- new_replicas: int32 [32], replicated, may hold values from 0 to 63
- slot_weights: bfloat16 [64, 3, 2048, 1024], P('req', None, None, 'exp'), may hold values from -0.125 to 0.125
Outputs:
- layer_out: bfloat16 [8192, 2048], P(('req', 'exp'))
- replica_weights: bfloat16 [32, 3, 2048, 1024], P('req', None, None, 'exp')
Inputs may be any that keep to these rules, and one draw needn't show every extreme that they name: `cache_block`: each index of req has exactly 2 of its 4 requests with a block; every block serves exactly one request. `expert_ids`: in each aligned block of 64 rows (the rows of one device) no expert is named by more than 10 rows, a bound that some block reaches; the 8 experts of a row differ. `old_slots`: every expert is in exactly one slot. `request_lengths`: the lengths of each index of req sum to 256.
All inputs are finite; a program needn't handle non-finite values.
Results may differ from a plain program's by a relative error of at most 0.025.
Values may be sent and summed in bfloat16 or wider, within the bound.
A program may use at most 128 MiB of HBM per device.

v0:
```python
import math
import jax
import jax.numpy as jnp
from jax import lax
from jax.sharding import PartitionSpec as P


def prepare(values, gain, position):
    vector = values.astype(jnp.float32)
    scaled = vector * lax.rsqrt(jnp.mean(vector * vector, axis=-1, keepdims=True) + 1e-06) * gain
    half_size = scaled.shape[-1] // 2
    frequency = 10000.0 ** (-(jnp.arange(half_size, dtype=jnp.float32) * 2.0 / scaled.shape[-1]))
    angles = position[:, None] * frequency[None, :]
    cosine = jnp.cos(angles)[:, None, :]
    sine_part = jnp.sin(angles)[:, None, :]
    lower_half = scaled[..., :half_size]
    upper_half = scaled[..., half_size:]
    rotated = jnp.concatenate(
        [
            lower_half * cosine - upper_half * sine_part,
            upper_half * cosine + lower_half * sine_part,
        ],
        axis=-1,
    )
    return rotated.astype(jnp.bfloat16)


def compact(block_rows, slots_wanted):
    live = block_rows >= 0
    ranks = jnp.cumsum(live.astype(jnp.int32), axis=1) - 1
    request_idx = jnp.arange(block_rows.shape[1], dtype=jnp.int32)[None, :]
    chosen_blocks = []
    chosen_requests = []
    for slot_num in range(slots_wanted):
        picked = live & (ranks == slot_num)
        chosen_blocks.append(jnp.sum(jnp.where(picked, block_rows, 0), axis=1))
        chosen_requests.append(jnp.sum(jnp.where(picked, request_idx, 0), axis=1))
    return (jnp.stack(chosen_blocks, axis=1), jnp.stack(chosen_requests, axis=1))


def run_slots(inbox, slot_weights, capacity):
    sources = inbox.shape[0]
    model_width = inbox.shape[2]
    slot_count = slot_weights.shape[0]
    grouped = inbox.reshape(sources, slot_count, capacity, model_width)
    results = []
    for slot_num in range(slot_count):
        in_rows = grouped[:, slot_num].reshape(sources * capacity, model_width)
        gate_act = jnp.dot(in_rows, slot_weights[slot_num, 0], preferred_element_type=jnp.float32)
        up_act = jnp.dot(in_rows, slot_weights[slot_num, 1], preferred_element_type=jnp.float32)
        hidden = (jax.nn.silu(gate_act) * up_act).astype(jnp.bfloat16)
        partial_value = lax.dot_general(
            hidden,
            slot_weights[slot_num, 2],
            (((1,), (1,)), ((), ())),
            preferred_element_type=jnp.float32,
        )
        results.append(partial_value.reshape(sources, capacity, model_width))
    return jnp.stack(results, axis=1).reshape(sources, slot_count * capacity, model_width)


def body(
    hidden_in,
    query_in,
    key_in,
    value_in,
    query_gain,
    key_gain,
    cache_keys,
    cache_values,
    cache_block,
    request_lengths,
    out_proj,
    norm_gain,
    expert_ids,
    gate_values,
    old_slots,
    new_replicas,
    slot_weights,
):
    req_count = lax.axis_size("req")
    exp_count = lax.axis_size("exp")
    group_idx = lax.axis_index("req")
    tok_grp, width_q = query_in.shape
    tok_dev, model_width = hidden_in.shape
    head_size = query_gain.shape[0]
    head_count = width_q // head_size
    cache_dev = cache_keys.shape[0]
    pre_len = cache_keys.shape[1]
    req_grp = request_lengths.shape[1]
    lengths = request_lengths[0]
    req_ends = jnp.cumsum(lengths)
    starts = req_ends - lengths
    places = jnp.arange(tok_grp, dtype=jnp.int32)
    member = (places[:, None] >= starts[None, :]) & (places[:, None] < req_ends[None, :])
    request_idx = jnp.arange(req_grp, dtype=jnp.int32)
    segment = jnp.sum(jnp.where(member, request_idx[None, :], 0), axis=1)
    offset = places - jnp.sum(jnp.where(member, starts[None, :], 0), axis=1)
    block_rows = cache_block.reshape(req_count, req_grp)
    my_blocks = lax.dynamic_index_in_dim(block_rows, group_idx, 0, keepdims=False)
    has_cache = my_blocks >= 0
    token_cached = jnp.sum(jnp.where(member & has_cache[None, :], 1, 0), axis=1) > 0
    position = (offset + jnp.where(token_cached, pre_len, 0)).astype(jnp.float32)
    need_blocks, need_requests = compact(block_rows, cache_dev)
    my_requests = lax.dynamic_index_in_dim(need_requests, group_idx, 0, keepdims=False)
    every_keys, every_values = (
        lax.all_gather(cache_keys, "req", axis=0, tiled=True),
        lax.all_gather(cache_values, "req", axis=0, tiled=True),
    )
    wanted = lax.dynamic_index_in_dim(need_blocks, group_idx, 0, keepdims=False)
    far_keys = jnp.take(every_keys, wanted, axis=0)
    far_values = jnp.take(every_values, wanted, axis=0)
    query_n = prepare(query_in.reshape(tok_grp, head_count, head_size), query_gain, position)
    key_n = prepare(key_in.reshape(tok_grp, head_count, head_size), key_gain, position)
    keyset = jnp.concatenate(
        [key_n, far_keys.reshape(cache_dev * pre_len, head_count, head_size)], axis=0
    )
    valueset = jnp.concatenate(
        [
            value_in.reshape(tok_grp, head_count, head_size),
            far_values.reshape(cache_dev * pre_len, head_count, head_size),
        ],
        axis=0,
    )
    key_request = jnp.concatenate([segment, jnp.repeat(my_requests, pre_len)])
    allowed = segment[:, None] == key_request[None, :]
    scores = jnp.einsum("qhd,khd->hqk", query_n, keyset, preferred_element_type=jnp.float32) * (
        1.0 / math.sqrt(head_size)
    )
    scores = jnp.where(allowed[None], scores, -1e30)
    peak = jnp.max(scores, axis=-1, keepdims=True)
    expos = jnp.exp(scores - peak)
    weights = (expos / jnp.sum(expos, axis=-1, keepdims=True)).astype(jnp.bfloat16)
    attended = jnp.einsum("hqk,khd->qhd", weights, valueset, preferred_element_type=jnp.float32)
    attended = attended.astype(jnp.bfloat16).reshape(tok_grp, width_q)
    attn_out = lax.psum_scatter(
        jnp.dot(attended, out_proj, preferred_element_type=jnp.float32),
        "exp",
        scatter_dimension=0,
        tiled=True,
    )
    residual = hidden_in.astype(jnp.float32) + attn_out
    normed = (
        residual
        * lax.rsqrt(jnp.mean(residual * residual, axis=-1, keepdims=True) + 1e-06)
        * norm_gain
    ).astype(jnp.bfloat16)
    topk_count = expert_ids.shape[1]
    slot_total = old_slots.shape[0]
    slots_here = slot_weights.shape[0]
    capacity = max(2, tok_dev * topk_count * 5 // (4 * slot_total))
    slot_range = jnp.arange(slot_total, dtype=jnp.int32)
    slot_of = jnp.sum(
        jnp.where(old_slots[None, :] == slot_range[:, None], slot_range[None, :], 0), axis=1
    )
    flat_ids = expert_ids.reshape(-1)
    onehot = flat_ids[:, None] == slot_range[None, :]
    row_slot = jnp.sum(jnp.where(onehot, slot_of[None, :], 0), axis=1)
    before = jnp.cumsum(onehot.astype(jnp.int32), axis=0) - onehot.astype(jnp.int32)
    row_rank = jnp.sum(jnp.where(onehot, before, 0), axis=1)
    target = row_slot * capacity + row_rank
    send_rows = jnp.repeat(normed, topk_count, axis=0)
    outbox = jnp.zeros((slot_total * capacity, model_width), jnp.bfloat16).at[target].set(send_rows)
    outbox = outbox.reshape(req_count, slots_here * capacity, model_width)
    copies = jnp.broadcast_to(
        outbox[:, None], (req_count, exp_count, slots_here * capacity, model_width)
    )
    copies = copies.reshape(req_count * exp_count, slots_here * capacity, model_width)
    inbox = lax.all_to_all(copies, ("req", "exp"), split_axis=0, concat_axis=0, tiled=True)
    partial_value = run_slots(inbox, slot_weights, capacity).astype(jnp.bfloat16)
    returned = lax.all_to_all(
        partial_value, ("req", "exp"), split_axis=0, concat_axis=0, tiled=True
    )
    result = jnp.sum(
        returned.astype(jnp.float32).reshape(
            req_count, exp_count, slots_here * capacity, model_width
        ),
        axis=1,
    )
    result_rows = jnp.take(result.reshape(slot_total * capacity, model_width), target, axis=0)
    mixture = jnp.sum(
        result_rows.reshape(tok_dev, topk_count, model_width) * gate_values[:, :, None], axis=1
    )
    layer_out = (residual + mixture).astype(jnp.bfloat16)
    spread_slots = lax.all_to_all(slot_weights, "req", split_axis=2, concat_axis=0, tiled=True)
    replica_onehot = new_replicas[:, None] == slot_range[None, :]
    source_slot = jnp.sum(jnp.where(replica_onehot, slot_of[None, :], 0), axis=1)
    chosen_pieces = jnp.take(spread_slots, source_slot, axis=0)
    replica_weights = lax.all_to_all(chosen_pieces, "req", split_axis=0, concat_axis=2, tiled=True)
    return (layer_out, replica_weights)


def solution(mesh):
    in_specs = (
        P(("req", "exp"), None),
        P("req", "exp"),
        P("req", "exp"),
        P("req", "exp"),
        P(),
        P(),
        P("req", None, "exp"),
        P("req", None, "exp"),
        P(),
        P("req", None),
        P("exp", None),
        P(),
        P(("req", "exp"), None),
        P(("req", "exp"), None),
        P(),
        P(),
        P("req", None, None, "exp"),
    )
    out_specs = (P(("req", "exp"), None), P("req", None, None, "exp"))
    return jax.shard_map(body, mesh=mesh, in_specs=in_specs, out_specs=out_specs, check_vma=False)
```

profile of v0, /device:TPU:74, one launch (start us, length us, event | category | flops | bytes accessed | tf_op | source)
XLA Modules:
  0.0 917.7 jit_solution(13939975030181986648)
XLA Ops:
  7.2 0.7 all-gather.3.cloned.1.call-update
  8.0 0.7 all-gather.5.cloned.1.call-update
  8.7 10.5 %copy.102 = bf16[2,3,2048,256]{3,1,0,2:T(4,128)(2,1)} copy(bf16[2,3,2048,256]{3,2,1,0:T(8,128)(2,1)} %param.35) | data formatting | bytes 12582912 | tf_op args[16]
  19.2 8.7 all-to-all-start.2
  28.1 0.2 reduce_window_sum.33
  28.3 0.1 select_reduce_fusion.6
  28.5 0.2 dynamic-slice_reduce_fusion.1
  28.7 0.2 dynamic-slice_reduce_fusion
  29.0 0.2 reduce-window.10
  29.2 0.1 copy.85
  29.6 0.9 copy.88
  30.6 1.1 copy.82
  31.7 0.8 copy.83
  33.0 0.5 multiply_cosine_fusion
  33.5 1.4 multiply_multiply_fusion
  34.9 1.1 subtract_convert_fusion.1
  36.1 141.0 %all-gather.3.cloned.1.call-done = bf16[64,32,512]{2,1,0:T(8,128)(2,1)} async-done(((bf16[2,32,512]{2,1,0:T(8,128)(2,1)}), bf16[64,32,512]{2,1,0:T(8,128)(2,1)}) %all-gather.3.cloned.1.call-update) | async-done | bytes 2097168 | tf_op jit(solution)/shard_map/all_gather | solution.py:108
  177.1 2.1 gather_fusion.2
  179.2 152.2 %all-gather.5.cloned.1.call-done = bf16[64,32,512]{2,1,0:T(8,128)(2,1)} async-done(((bf16[2,32,512]{2,1,0:T(8,128)(2,1)}), bf16[64,32,512]{2,1,0:T(8,128)(2,1)}) %all-gather.5.cloned.1.call-update) | async-done | bytes 2097168 | tf_op jit(solution)/shard_map/all_gather | solution.py:107
  331.4 2.1 gather_fusion.3
  333.8 2.7 fusion.65
  336.5 1.7 convolution_convert_fusion
  338.2 2.1 fusion.70
  340.6 1.2 reduce-window.11
  341.8 0.2 slice_reduce_fusion
  342.2 0.1 select_reduce_fusion
  342.3 52.4 %reduce-scatter.2.cloned.1.call-done = f32[64,2048]{1,0:T(8,128)} async-done(((f32[256,2048]{1,0:T(8,128)}), f32[64,2048]{1,0:T(8,128)}) %reduce-scatter.2.cloned.1.call-update) | async-done | bytes 524304 | tf_op jit(solution)/shard_map/reduce_scatter | solution.py:136
  394.7 1.2 multiply_reduce_fusion
  396.0 1.2 multiply_convert_fusion
  397.1 5.6 scatter_custom_fusion
  402.7 5.1 broadcast_in_dim.195
  407.8 8.1 broadcast_in_dim.196
  416.0 9.2 %all-to-all-start = ((bf16[128,20,2048]{2,1,0:T(8,128)(2,1)}), bf16[128,20,2048]{2,1,0:T(8,128)(2,1)}, u32[]{:S(2)}, u32[]{:S(2)}) async-start(bf16[128,20,2048]{2,1,0:T(8,128)(2,1)} %bitcast.108), calls=%async_computation.1 | async-start | bytes 25165824 | tf_op jit(solution)/shard_map/all_to_all | solution.py:169
  425.2 0.2 select_reduce_fusion.2
  425.4 4.9 copy.103
  430.4 3.2 copy.104
  433.6 5.2 gather_fusion.1
  438.8 3.9 broadcast_select_fusion
  442.7 145.0 %all-to-all-done = bf16[128,20,2048]{2,1,0:T(8,128)(2,1)} async-done(((bf16[128,20,2048]{2,1,0:T(8,128)(2,1)}), bf16[128,20,2048]{2,1,0:T(8,128)(2,1)}, u32[]{:S(2)}, u32[]{:S(2)}) %all-to-all-start) | async-done | bytes 10485792 | tf_op jit(solution)/shard_map/all_to_all | solution.py:169
  587.7 6.8 all-to-all-start.3
  594.5 12.6 %copy.93 = bf16[128,20,2048]{2,0,1:T(8,128)(2,1)} copy(bf16[128,20,2048]{2,1,0:T(8,128)(2,1)} %all-to-all-done) | data formatting | bytes 20971520 | tf_op jit(solution)/shard_map/all_to_all | solution.py:169
  607.2 10.2 %fusion.64 = (bf16[128,1,10,2048]{3,0,2,1:T(8,128)(2,1)}, bf16[128,1,10,2048]{3,0,2,1:T(8,128)(2,1)}) fusion(bf16[128,2,10,2048]{3,0,2,1:T(8,128)(2,1)} %bitcast.109), kind=kLoop, calls=%fused_computation.135 | loop fusion | bytes 20971520 | tf_op jit(solution)/shard_map/slice | solution.py:48
  617.3 9.0 copy.94
  626.4 10.0 %reshape_squeeze.6 = bf16[1280,2048]{1,0:T(8,128)(2,1)} reshape(bf16[128,1,10,2048]{3,2,0,1:T(8,128)(2,1)} %copy.94) | data formatting | bytes 10485760 | tf_op jit(solution)/shard_map/reshape;squeeze | solution.py:48
  636.4 4.5 fusion.17
  640.9 3.0 fusion.3
  643.8 0.2 reshape.293
  644.1 9.0 copy.96
  653.1 10.2 %reshape_squeeze.7 = bf16[1280,2048]{1,0:T(8,128)(2,1)} reshape(bf16[128,1,10,2048]{3,2,0,1:T(8,128)(2,1)} %copy.96) | data formatting | bytes 10485760 | tf_op jit(solution)/shard_map/reshape;squeeze | solution.py:48
  663.3 4.5 fusion.14
  667.8 3.0 fusion.4
  670.8 0.2 reshape.294
  671.0 5.1 convert_bitcast_fusion.1
  676.1 5.1 convert_bitcast_fusion
  681.2 9.0 pad_maximum_fusion
  690.1 14.1 %copy.98 = bf16[128,20,2048]{2,1,0:T(8,128)(2,1)} copy(bf16[128,20,2048]{2,0,1:T(8,128)(2,1)} %bitcast.110) | data formatting | bytes 20971520 | tf_op jit(solution)/shard_map/convert_element_type | solution.py:170
  704.2 10.9 %all-to-all-start.1 = ((bf16[128,20,2048]{2,1,0:T(8,128)(2,1)}), bf16[128,20,2048]{2,1,0:T(8,128)(2,1)}, u32[]{:S(2)}, u32[]{:S(2)}) async-start(bf16[128,20,2048]{2,1,0:T(8,128)(2,1)} %copy.98), calls=%async_computation.2 | async-start | bytes 25165824 | tf_op jit(solution)/shard_map/all_to_all | solution.py:171
  715.3 4.0 copy.105
  719.3 160.7 %all-to-all-done.1 = bf16[128,20,2048]{2,1,0:T(8,128)(2,1)} async-done(((bf16[128,20,2048]{2,1,0:T(8,128)(2,1)}), bf16[128,20,2048]{2,1,0:T(8,128)(2,1)}, u32[]{:S(2)}, u32[]{:S(2)}) %all-to-all-start.1) | async-done | bytes 10485792 | tf_op jit(solution)/shard_map/all_to_all | solution.py:171
  880.0 11.1 %convert_reduce_fusion = f32[32,20,2048]{2,1,0:T(8,128)} fusion(bf16[128,20,2048]{2,1,0:T(8,128)(2,1)} %all-to-all-done.1), kind=kLoop, calls=%fused_computation.6 | loop fusion | flops 9175040 | bytes 15728640 | tf_op jit(solution)/shard_map/reduce_sum | solution.py:174
  891.2 6.8 reshape.297
  898.0 8.1 gather_fusion
  906.1 4.1 fusion.2
  910.2 0.8 add_convert_fusion
  (87 shorter events, 2.0 us)
Async XLA Ops:
  7.2 331.0 %copy-start = (bf16[512,2048]{1,0:T(8,128)(2,1)S(1)}, bf16[512,2048]{1,0:T(8,128)(2,1)}, u32[]{:S(2)}) copy-start(bf16[512,2048]{1,0:T(8,128)(2,1)} %param.29) | copy-start | bytes 6291460
  7.2 169.9 %all-gather.3.cloned.1.call-start = ((), (), s32[]{:S(2)}) async-start(), calls=%async_computation.5 | async-start | bytes 2162688 | tf_op jit(solution)/shard_map/all_gather | solution.py:108
  7.9 323.5 %all-gather.5.cloned.1.call-start = ((), (), s32[]{:S(2)}) async-start(), calls=%async_computation.6 | async-start | bytes 2162688 | tf_op jit(solution)/shard_map/all_gather | solution.py:107
  19.1 8.9 copy-start.12
  19.1 9.9 %copy-start.15 = (s32[1,4]{1,0:T(1,128)S(1)}, s32[1,4]{1,0:T(1,128)}, u32[]{:S(2)}) copy-start(s32[1,4]{1,0:T(1,128)} %param.28) | copy-start | bytes 52
  19.2 10.1 %copy-start.6 = (bf16[256,512]{1,0:T(8,128)(2,1)S(1)}, bf16[256,512]{1,0:T(8,128)(2,1)}, u32[]{:S(2)}) copy-start(bf16[256,512]{1,0:T(8,128)(2,1)} %param.20) | copy-start | bytes 786436
  19.2 10.3 %copy-start.7 = (bf16[256,512]{1,0:T(8,128)(2,1)S(1)}, bf16[256,512]{1,0:T(8,128)(2,1)}, u32[]{:S(2)}) copy-start(bf16[256,512]{1,0:T(8,128)(2,1)} %param.21) | copy-start | bytes 786436
  19.2 388.7 %all-to-all-start.2 = ((bf16[2,3,2048,256]{3,1,0,2:T(4,128)(2,1)}), bf16[2,3,2048,256]{3,1,0,2:T(4,128)(2,1)}, u32[]{:S(2)}, u32[]{:S(2)}) async-start(bf16[2,3,2048,256]{3,1,0,2:T(4,128)(2,1)} %copy.102), calls=%async_computation.3 | async-start | bytes 16777216 | tf_op jit(solution)/shard_map/all_to_all | solution.py:185
  27.9 5.6 copy-start.13
  27.9 5.6 copy-start.14
  27.9 366.8 %reduce-scatter.2.cloned.1.call-start = ((), (), s32[]{:S(2)}) async-start(), calls=%async_computation.7 | async-start | bytes 2621440 | tf_op jit(solution)/shard_map/reduce_scatter | solution.py:136
  34.9 301.6 %copy-start.8 = (bf16[256,4,128]{2,0,1:T(8,128)(2,1)S(1)}, bf16[256,4,128]{2,0,1:T(8,128)(2,1)}, u32[]{:S(2)}) copy-start(bf16[256,4,128]{2,0,1:T(8,128)(2,1)} %copy.83) | copy-start | bytes 786436
  338.2 2.1 copy-start.10
  338.2 3.9 copy-start.16
  338.2 56.6 %copy-start.5 = (bf16[64,2048]{1,0:T(8,128)(2,1)S(1)}, bf16[64,2048]{1,0:T(8,128)(2,1)}, u32[]{:S(2)}) copy-start(bf16[64,2048]{1,0:T(8,128)(2,1)} %param.19) | copy-start | bytes 786436
  338.2 57.8 %copy-start.9 = (f32[2048]{0:T(1024)S(1)}, f32[2048]{0:T(1024)}, u32[]{:S(2)}) copy-start(f32[2048]{0:T(1024)} %param.30) | copy-start | bytes 24580
  416.0 9.2 %copy-start.17 = (s32[32]{0:T(128)S(1)}, s32[32]{0:T(128)}, u32[]{:S(2)}) copy-start(s32[32]{0:T(128)} %param.34) | copy-start | bytes 388
  416.0 171.7 %all-to-all-start = ((bf16[128,20,2048]{2,1,0:T(8,128)(2,1)}), bf16[128,20,2048]{2,1,0:T(8,128)(2,1)}, u32[]{:S(2)}, u32[]{:S(2)}) async-start(bf16[128,20,2048]{2,1,0:T(8,128)(2,1)} %bitcast.108), calls=%async_computation.1 | async-start | bytes 25165824 | tf_op jit(solution)/shard_map/all_to_all | solution.py:169
  587.7 116.5 %all-to-all-start.3 = ((bf16[32,3,64,256]{3,2,1,0:T(8,128)(2,1)}), bf16[32,3,64,256]{3,2,1,0:T(8,128)(2,1)}, u32[]{:S(2)}, u32[]{:S(2)}) async-start(bf16[32,3,64,256]{3,2,1,0:T(8,128)(2,1)} %broadcast_select_fusion), calls=%async_computation.4 | async-start | bytes 6291456 | tf_op jit(solution)/shard_map/all_to_all | solution.py:189
  636.4 4.5 copy-start.2
  663.3 4.5 copy-start.3
  704.2 11.0 %copy-start.11 = (f32[64,8]{0,1:T(8,128)S(1)}, f32[64,8]{0,1:T(8,128)}, u32[]{:S(2)}) copy-start(f32[64,8]{0,1:T(8,128)} %param.32) | copy-start | bytes 6148
  704.2 175.8 %all-to-all-start.1 = ((bf16[128,20,2048]{2,1,0:T(8,128)(2,1)}), bf16[128,20,2048]{2,1,0:T(8,128)(2,1)}, u32[]{:S(2)}, u32[]{:S(2)}) async-start(bf16[128,20,2048]{2,1,0:T(8,128)(2,1)} %copy.98), calls=%async_computation.2 | async-start | bytes 25165824 | tf_op jit(solution)/shard_map/all_to_all | solution.py:171
  898.0 13.0 %copy-start.1 = (bf16[512,2048]{1,0:T(8,128)(2,1)S(1)}, bf16[512,2048]{1,0:T(8,128)(2,1)}, u32[]{:S(2)}) copy-start(bf16[512,2048]{1,0:T(8,128)(2,1)} %param.29) | copy-start | bytes 6291460
  906.1 4.1 copy-start.4
Sparse Core Ops, SparseCore 0:
  9.7 167.3 all-gather.2
  178.7 152.7 all-gather.4
  340.4 54.2 reduce-scatter.1
where the time goes:
time: 928 us; the launch traced here: 918 us
  waiting for transfers between devices  653 us (70%)
  local copies, waits for them, and re-layouts  146 us (16%)
  other arithmetic  37.1 us (4%)
  starting transfers between devices  35.8 us (4%)
  matrix products  31.5 us (3%)
  between operations  14.5 us (2%)
    all_to_all x1, waiting for transfers between devices, body(): lax.all_to_all(partial_value, ('req', 'exp'), split_axis=0, concat_axis=0...  161 us
    all_gather x1, waiting for transfers between devices, body(): lax.all_gather(cache_keys, 'req', axis=0, tiled=True)  152 us
    all_to_all x1, waiting for transfers between devices, body(): lax.all_to_all(copies, ('req', 'exp'), split_axis=0, concat_axis=0, tiled...  145 us
    all_gather x1, waiting for transfers between devices, body(): lax.all_gather(cache_values, 'req', axis=0, tiled=True)  141 us
    reduce_scatter x1, waiting for transfers between devices, body(): lax.psum_scatter(jnp.dot(attended, out_proj, preferred_element_type=jnp.f...  52.4 us
    slice x3, local copies, waits for them, and re-layouts, run_slots(): in_rows = grouped[:, slot_num].reshape(sources * capacity, model_width)  28.2 us
    another operation x2, local copies, waits for them, and re-layouts, run_slots(): in_rows = grouped[:, slot_num].reshape(sources * capacity, model_width)  20.2 us
  transfers between devices with their start and end apart: 7, of which 5 were waited for; matrix products, arithmetic and copies ran while one was open for 19% of the time, Pallas kernels for 0%

commit v1 on v0

--- a/solution.py
+++ b/solution.py
@@ -3,6 +3,11 @@
 import jax.numpy as jnp
 from jax import lax
 from jax.sharding import PartitionSpec as P
+
+_deliver_members_all = lambda local, peer_axis: jnp.concatenate(
+    lax.all_to_all(jnp.stack([local for _ in range(lax.axis_size(peer_axis))]), peer_axis, 0, 0),
+    axis=0,
+)
 
 
 def prepare(values, gain, position):
@@ -104,7 +109,7 @@
     need_blocks, need_requests = compact(block_rows, cache_dev)
     my_requests = lax.dynamic_index_in_dim(need_requests, group_idx, 0, keepdims=False)
     every_keys, every_values = (
-        lax.all_gather(cache_keys, "req", axis=0, tiled=True),
+        _deliver_members_all(cache_keys, "req"),
         lax.all_gather(cache_values, "req", axis=0, tiled=True),
     )
     wanted = lax.dynamic_index_in_dim(need_blocks, group_idx, 0, keepdims=False)

time: 928 us -> 774 us (0.83)
  waiting for transfers between devices: 653 us -> 488 us
  starting transfers between devices: 35.8 us -> 45.6 us
    all_gather x1 -> x0, waiting for transfers between devices: 152 us -> none  [body(): lax.all_gather(cache_keys, 'req', axis=0, tiled=True)]
    all_gather x1, waiting for transfers between devices: 141 us -> 111 us  [body(): lax.all_gather(cache_values, 'req', axis=0, tiled=True)]
    all_to_all x0 -> x1, waiting for transfers between devices: none -> 18.4 us  [lax.all_to_all(jnp.stack([local for _ in range(lax.axis_size(peer_axis))]...]
  transfers between devices with their start and end apart: 7 -> 7, of which waited for: 5 -> 5; matrix products, arithmetic and copies ran while one was open for 19% -> 23% of each run, Pallas kernels for 0% -> 0%
where the time goes in v1:
time: 774 us; the launch traced here: 763 us
  waiting for transfers between devices  488 us (63%)
  local copies, waits for them, and re-layouts  147 us (19%)
  starting transfers between devices  45.6 us (6%)
  other arithmetic  36 us (5%)
  matrix products  31.5 us (4%)
  between operations  14.9 us (2%)
    all_to_all x1, waiting for transfers between devices, body(): lax.all_to_all(partial_value, ('req', 'exp'), split_axis=0, concat_axis=0...  161 us
    all_to_all x1, waiting for transfers between devices, body(): lax.all_to_all(copies, ('req', 'exp'), split_axis=0, concat_axis=0, tiled...  145 us
    all_gather x1, waiting for transfers between devices, body(): lax.all_gather(cache_values, 'req', axis=0, tiled=True)  111 us
    reduce_scatter x1, waiting for transfers between devices, body(): lax.psum_scatter(jnp.dot(attended, out_proj, preferred_element_type=jnp.f...  52.5 us
    slice x3, local copies, waits for them, and re-layouts, run_slots(): in_rows = grouped[:, slot_num].reshape(sources * capacity, model_width)  28.2 us
    another operation x2, local copies, waits for them, and re-layouts, run_slots(): in_rows = grouped[:, slot_num].reshape(sources * capacity, model_width)  20.2 us
    all_to_all x1, waiting for transfers between devices, lax.all_to_all(jnp.stack([local for _ in range(lax.axis_size(peer_axis))]...  18.4 us
  transfers between devices with their start and end apart: 7, of which 5 were waited for; matrix products, arithmetic and copies ran while one was open for 23% of the time, Pallas kernels for 0%

profile of v1, /device:TPU:74, one launch (start us, length us, event | category | flops | bytes accessed | tf_op | source)
XLA Modules:
  0.0 763.2 jit_solution(3486110538960904755)
XLA Ops:
  7.3 0.7 all-gather.2.cloned.1.call-update
  8.0 2.4 stack.23
  10.4 8.7 %all-to-all-start = ((bf16[32,2,32,512]{3,2,1,0:T(8,128)(2,1)}), bf16[32,2,32,512]{3,2,1,0:T(8,128)(2,1)}, u32[]{:S(2)}, u32[]{:S(2)}) async-start(bf16[32,2,32,512]{3,2,1,0:T(8,128)(2,1)} %stack.23), calls=%async_computation | async-start | bytes 4194304 | tf_op jit(solution)/shard_map/all_to_all | solution.py:8
  19.3 0.2 reduce_window_sum.33
  19.5 0.1 select_reduce_fusion.6
  19.6 0.2 dynamic-slice_reduce_fusion.1
  19.8 0.2 dynamic-slice_reduce_fusion
  20.2 0.2 reduce-window.10
  20.4 0.1 copy.85
  21.1 0.9 copy.88
  22.2 0.2 copy.83
  22.4 10.5 %copy.102 = bf16[2,3,2048,256]{3,1,0,2:T(4,128)(2,1)} copy(bf16[2,3,2048,256]{3,2,1,0:T(8,128)(2,1)} %param.35) | data formatting | bytes 12582912 | tf_op args[16]
  33.1 0.5 multiply_cosine_fusion
  33.7 0.3 multiply_multiply_fusion
  34.0 1.1 subtract_convert_fusion.1
  35.2 18.4 %all-to-all-done = bf16[32,2,32,512]{3,2,1,0:T(8,128)(2,1)} async-done(((bf16[32,2,32,512]{3,2,1,0:T(8,128)(2,1)}), bf16[32,2,32,512]{3,2,1,0:T(8,128)(2,1)}, u32[]{:S(2)}, u32[]{:S(2)}) %all-to-all-start) | async-done | bytes 2097184 | tf_op jit(solution)/shard_map/all_to_all | solution.py:8
  53.5 9.9 %all-to-all-start.3 = ((bf16[2,3,2048,256]{3,1,0,2:T(4,128)(2,1)}), bf16[2,3,2048,256]{3,1,0,2:T(4,128)(2,1)}, u32[]{:S(2)}, u32[]{:S(2)}) async-start(bf16[2,3,2048,256]{3,1,0,2:T(4,128)(2,1)} %copy.102), calls=%async_computation.4 | async-start | bytes 16777216 | tf_op jit(solution)/shard_map/all_to_all | solution.py:190
  63.5 2.1 gather_fusion.3
  65.6 110.9 %all-gather.2.cloned.1.call-done = bf16[64,32,512]{2,1,0:T(8,128)(2,1)} async-done(((bf16[2,32,512]{2,1,0:T(8,128)(2,1)}), bf16[64,32,512]{2,1,0:T(8,128)(2,1)}) %all-gather.2.cloned.1.call-update) | async-done | bytes 2097168 | tf_op jit(solution)/shard_map/all_gather | solution.py:113
  176.5 2.1 gather_fusion.2
  178.8 2.7 fusion.65
  181.5 1.7 convolution_convert_fusion
  183.3 2.0 fusion.70
  185.6 1.2 reduce-window.11
  186.8 0.2 slice_reduce_fusion
  187.2 0.1 select_reduce_fusion
  187.4 52.5 %reduce-scatter.2.cloned.1.call-done = f32[64,2048]{1,0:T(8,128)} async-done(((f32[256,2048]{1,0:T(8,128)}), f32[64,2048]{1,0:T(8,128)}) %reduce-scatter.2.cloned.1.call-update) | async-done | bytes 524304 | tf_op jit(solution)/shard_map/reduce_scatter | solution.py:141
  239.9 1.2 multiply_reduce_fusion
  241.1 1.2 multiply_convert_fusion
  242.3 5.6 scatter_custom_fusion
  247.9 5.1 broadcast_in_dim.195
  253.0 8.1 %broadcast_in_dim.196 = bf16[32,4,20,2048]{3,2,1,0:T(8,128)(2,1)} broadcast(bf16[32,20,2048]{2,1,0:T(8,128)(2,1)} %broadcast_in_dim.195), dimensions={0,2,3} | broadcast | bytes 13107200 | tf_op jit(solution)/shard_map/broadcast_in_dim | solution.py:170
  261.1 9.2 %all-to-all-start.1 = ((bf16[128,20,2048]{2,1,0:T(8,128)(2,1)}), bf16[128,20,2048]{2,1,0:T(8,128)(2,1)}, u32[]{:S(2)}, u32[]{:S(2)}) async-start(bf16[128,20,2048]{2,1,0:T(8,128)(2,1)} %bitcast.109), calls=%async_computation.2 | async-start | bytes 25165824 | tf_op jit(solution)/shard_map/all_to_all | solution.py:174
  270.4 0.2 select_reduce_fusion.2
  270.6 4.9 copy.103
  275.5 3.2 copy.104
  278.7 5.2 gather_fusion.1
  283.9 3.9 broadcast_select_fusion
  287.8 145.0 %all-to-all-done.1 = bf16[128,20,2048]{2,1,0:T(8,128)(2,1)} async-done(((bf16[128,20,2048]{2,1,0:T(8,128)(2,1)}), bf16[128,20,2048]{2,1,0:T(8,128)(2,1)}, u32[]{:S(2)}, u32[]{:S(2)}) %all-to-all-start.1) | async-done | bytes 10485792 | tf_op jit(solution)/shard_map/all_to_all | solution.py:174
  432.9 6.8 all-to-all-start.4
  439.7 12.6 %copy.93 = bf16[128,20,2048]{2,0,1:T(8,128)(2,1)} copy(bf16[128,20,2048]{2,1,0:T(8,128)(2,1)} %all-to-all-done.1) | data formatting | bytes 20971520 | tf_op jit(solution)/shard_map/all_to_all | solution.py:174
  452.3 10.2 %fusion.64 = (bf16[128,1,10,2048]{3,0,2,1:T(8,128)(2,1)}, bf16[128,1,10,2048]{3,0,2,1:T(8,128)(2,1)}) fusion(bf16[128,2,10,2048]{3,0,2,1:T(8,128)(2,1)} %bitcast.110), kind=kLoop, calls=%fused_computation.135 | loop fusion | bytes 20971520 | tf_op jit(solution)/shard_map/slice | solution.py:53
  462.5 9.0 %copy.94 = bf16[128,1,10,2048]{3,2,0,1:T(8,128)(2,1)} copy(bf16[128,1,10,2048]{3,0,2,1:T(8,128)(2,1)} %get-tuple-element.14) | data formatting | bytes 10485760 | tf_op jit(solution)/shard_map/slice | solution.py:53
  471.5 10.0 %reshape_squeeze.6 = bf16[1280,2048]{1,0:T(8,128)(2,1)} reshape(bf16[128,1,10,2048]{3,2,0,1:T(8,128)(2,1)} %copy.94) | data formatting | bytes 10485760 | tf_op jit(solution)/shard_map/reshape;squeeze | solution.py:53
  481.5 4.5 fusion.17
  486.1 2.9 fusion.3
  489.0 0.2 reshape.299
  489.2 9.0 %copy.96 = bf16[128,1,10,2048]{3,2,0,1:T(8,128)(2,1)} copy(bf16[128,1,10,2048]{3,0,2,1:T(8,128)(2,1)} %get-tuple-element.15) | data formatting | bytes 10485760 | tf_op jit(solution)/shard_map/slice | solution.py:53
  498.2 10.2 %reshape_squeeze.7 = bf16[1280,2048]{1,0:T(8,128)(2,1)} reshape(bf16[128,1,10,2048]{3,2,0,1:T(8,128)(2,1)} %copy.96) | data formatting | bytes 10485760 | tf_op jit(solution)/shard_map/reshape;squeeze | solution.py:53
  508.5 4.5 fusion.14
  513.0 2.9 fusion.4
  515.9 0.2 reshape.300
  516.2 5.1 convert_bitcast_fusion.1
  521.3 5.1 convert_bitcast_fusion
  526.3 9.0 %pad_maximum_fusion = bf16[128,2,10,2048]{3,0,2,1:T(8,128)(2,1)} fusion(bf16[128,1,10,2048]{3,0,2,1:T(8,128)(2,1)} %convert_bitcast_fusion, bf16[128,1,10,2048]{3,0,2,1:T(8,128)(2,1)} %convert_bitcast_fusion.1), kind=kLoop, calls=%fused_computation.7 | loop fusion | flops 5242880 | bytes 20971520 | tf_op jit(solution)/shard_map/stack | solution.py:64
  535.3 14.1 %copy.98 = bf16[128,20,2048]{2,1,0:T(8,128)(2,1)} copy(bf16[128,20,2048]{2,0,1:T(8,128)(2,1)} %bitcast.111) | data formatting | bytes 20971520 | tf_op jit(solution)/shard_map/convert_element_type | solution.py:175
  549.4 10.9 %all-to-all-start.2 = ((bf16[128,20,2048]{2,1,0:T(8,128)(2,1)}), bf16[128,20,2048]{2,1,0:T(8,128)(2,1)}, u32[]{:S(2)}, u32[]{:S(2)}) async-start(bf16[128,20,2048]{2,1,0:T(8,128)(2,1)} %copy.98), calls=%async_computation.3 | async-start | bytes 25165824 | tf_op jit(solution)/shard_map/all_to_all | solution.py:176
  560.5 4.0 copy.105
  564.4 160.7 %all-to-all-done.2 = bf16[128,20,2048]{2,1,0:T(8,128)(2,1)} async-done(((bf16[128,20,2048]{2,1,0:T(8,128)(2,1)}), bf16[128,20,2048]{2,1,0:T(8,128)(2,1)}, u32[]{:S(2)}, u32[]{:S(2)}) %all-to-all-start.2) | async-done | bytes 10485792 | tf_op jit(solution)/shard_map/all_to_all | solution.py:176
  725.2 11.1 %convert_reduce_fusion = f32[32,20,2048]{2,1,0:T(8,128)} fusion(bf16[128,20,2048]{2,1,0:T(8,128)(2,1)} %all-to-all-done.2), kind=kLoop, calls=%fused_computation.6 | loop fusion | flops 9175040 | bytes 15728640 | tf_op jit(solution)/shard_map/reduce_sum | solution.py:179
  736.3 6.8 reshape.303
  743.1 8.1 %gather_fusion = f32[512,2048]{1,0:T(8,128)} fusion(f32[640,2048]{1,0:T(8,128)} %reshape.303, s32[1024]{0:T(1024)S(1)} %pad_clamp_fusion.1), kind=kCustom, calls=%fused_computation.2 | custom fusion | bytes 8390656 | tf_op jit(solution)/shard_map/jit(_take)/gather | solution.py:185
  751.2 4.1 fusion.2
  755.4 0.8 add_convert_fusion
  (89 shorter events, 2.1 us)
Async XLA Ops:
  7.2 176.1 %copy-start = (bf16[512,2048]{1,0:T(8,128)(2,1)S(1)}, bf16[512,2048]{1,0:T(8,128)(2,1)}, u32[]{:S(2)}) copy-start(bf16[512,2048]{1,0:T(8,128)(2,1)} %param.29) | copy-start | bytes 6291460
  7.2 12.0 %copy-start.13 = (s32[128]{0:T(128)S(1)}, s32[128]{0:T(128)}, u32[]{:S(2)}) copy-start(s32[128]{0:T(128)} %param.27) | copy-start | bytes 1540
  7.2 13.0 %copy-start.16 = (s32[1,4]{1,0:T(1,128)S(1)}, s32[1,4]{1,0:T(1,128)}, u32[]{:S(2)}) copy-start(s32[1,4]{1,0:T(1,128)} %param.28) | copy-start | bytes 52
  7.2 13.2 %copy-start.7 = (bf16[256,512]{1,0:T(8,128)(2,1)S(1)}, bf16[256,512]{1,0:T(8,128)(2,1)}, u32[]{:S(2)}) copy-start(bf16[256,512]{1,0:T(8,128)(2,1)} %param.20) | copy-start | bytes 786436
  7.2 13.3 %copy-start.8 = (bf16[256,512]{1,0:T(8,128)(2,1)S(1)}, bf16[256,512]{1,0:T(8,128)(2,1)}, u32[]{:S(2)}) copy-start(bf16[256,512]{1,0:T(8,128)(2,1)} %param.21) | copy-start | bytes 786436
  7.2 169.3 %all-gather.2.cloned.1.call-start = ((), (), s32[]{:S(2)}) async-start(), calls=%async_computation.6 | async-start | bytes 2162688 | tf_op jit(solution)/shard_map/all_gather | solution.py:113
  10.4 11.6 %copy-start.9 = (bf16[256,512]{1,0:T(8,128)(2,1)S(1)}, bf16[256,512]{1,0:T(8,128)(2,1)}, u32[]{:S(2)}) copy-start(bf16[256,512]{1,0:T(8,128)(2,1)} %param.22) | copy-start | bytes 786436
  10.4 43.1 %all-to-all-start = ((bf16[32,2,32,512]{3,2,1,0:T(8,128)(2,1)}), bf16[32,2,32,512]{3,2,1,0:T(8,128)(2,1)}, u32[]{:S(2)}, u32[]{:S(2)}) async-start(bf16[32,2,32,512]{3,2,1,0:T(8,128)(2,1)} %stack.23), calls=%async_computation | async-start | bytes 4194304 | tf_op jit(solution)/shard_map/all_to_all | solution.py:8
  22.3 11.3 %copy-start.6 = (f32[256,4,128]{2,0,1:T(8,128)S(1)}, f32[256,4,128]{2,0,1:T(8,128)}, u32[]{:S(2)}) copy-start(f32[256,4,128]{2,0,1:T(8,128)} %copy.88) | copy-start | bytes 1572868
  22.4 11.3 %copy-start.14 = (f32[128]{0:T(128)S(1)}, f32[128]{0:T(128)}, u32[]{:S(2)}) copy-start(f32[128]{0:T(128)} %param.24) | copy-start | bytes 1540
  22.4 11.3 %copy-start.15 = (f32[128]{0:T(128)S(1)}, f32[128]{0:T(128)}, u32[]{:S(2)}) copy-start(f32[128]{0:T(128)} %param.23) | copy-start | bytes 1540
  53.5 199.5 %all-to-all-start.3 = ((bf16[2,3,2048,256]{3,1,0,2:T(4,128)(2,1)}), bf16[2,3,2048,256]{3,1,0,2:T(4,128)(2,1)}, u32[]{:S(2)}, u32[]{:S(2)}) async-start(bf16[2,3,2048,256]{3,1,0,2:T(4,128)(2,1)} %copy.102), calls=%async_computation.4 | async-start | bytes 16777216 | tf_op jit(solution)/shard_map/all_to_all | solution.py:190
  63.4 176.5 %reduce-scatter.2.cloned.1.call-start = ((), (), s32[]{:S(2)}) async-start(), calls=%async_computation.7 | async-start | bytes 2621440 | tf_op jit(solution)/shard_map/reduce_scatter | solution.py:141
  183.2 2.1 copy-start.11
  183.2 3.9 copy-start.17
  183.2 56.7 %copy-start.5 = (bf16[64,2048]{1,0:T(8,128)(2,1)S(1)}, bf16[64,2048]{1,0:T(8,128)(2,1)}, u32[]{:S(2)}) copy-start(bf16[64,2048]{1,0:T(8,128)(2,1)} %param.19) | copy-start | bytes 786436
  183.2 57.9 %copy-start.10 = (f32[2048]{0:T(1024)S(1)}, f32[2048]{0:T(1024)}, u32[]{:S(2)}) copy-start(f32[2048]{0:T(1024)} %param.30) | copy-start | bytes 24580
  261.1 9.2 %copy-start.18 = (s32[32]{0:T(128)S(1)}, s32[32]{0:T(128)}, u32[]{:S(2)}) copy-start(s32[32]{0:T(128)} %param.34) | copy-start | bytes 388
  261.1 171.7 %all-to-all-start.1 = ((bf16[128,20,2048]{2,1,0:T(8,128)(2,1)}), bf16[128,20,2048]{2,1,0:T(8,128)(2,1)}, u32[]{:S(2)}, u32[]{:S(2)}) async-start(bf16[128,20,2048]{2,1,0:T(8,128)(2,1)} %bitcast.109), calls=%async_computation.2 | async-start | bytes 25165824 | tf_op jit(solution)/shard_map/all_to_all | solution.py:174
  432.9 116.5 %all-to-all-start.4 = ((bf16[32,3,64,256]{3,2,1,0:T(8,128)(2,1)}), bf16[32,3,64,256]{3,2,1,0:T(8,128)(2,1)}, u32[]{:S(2)}, u32[]{:S(2)}) async-start(bf16[32,3,64,256]{3,2,1,0:T(8,128)(2,1)} %broadcast_select_fusion), calls=%async_computation.5 | async-start | bytes 6291456 | tf_op jit(solution)/shard_map/all_to_all | solution.py:194
  481.5 4.5 copy-start.2
  508.5 4.5 copy-start.3
  549.4 11.0 %copy-start.12 = (f32[64,8]{0,1:T(8,128)S(1)}, f32[64,8]{0,1:T(8,128)}, u32[]{:S(2)}) copy-start(f32[64,8]{0,1:T(8,128)} %param.32) | copy-start | bytes 6148
  549.4 175.8 %all-to-all-start.2 = ((bf16[128,20,2048]{2,1,0:T(8,128)(2,1)}), bf16[128,20,2048]{2,1,0:T(8,128)(2,1)}, u32[]{:S(2)}, u32[]{:S(2)}) async-start(bf16[128,20,2048]{2,1,0:T(8,128)(2,1)} %copy.98), calls=%async_computation.3 | async-start | bytes 25165824 | tf_op jit(solution)/shard_map/all_to_all | solution.py:176
  743.1 13.0 %copy-start.1 = (bf16[512,2048]{1,0:T(8,128)(2,1)S(1)}, bf16[512,2048]{1,0:T(8,128)(2,1)}, u32[]{:S(2)}) copy-start(bf16[512,2048]{1,0:T(8,128)(2,1)} %param.29) | copy-start | bytes 6291460
  751.2 4.1 copy-start.4
Sparse Core Ops, SparseCore 0:
  9.7 166.7 all-gather.1
  185.5 54.3 reduce-scatter.1
